TPU v7x, 256 devices: a whole 4x4x8 slice. The times are simulated.
256 devices in a mesh: seg: 32 (over y, x, core), fsdp: 8 (over z).
Axes of the slice: x: 4, y: 4, z: 8, core: 2. Of those that a mesh axis runs over, the one named last changes fastest.
Arguments:
- tokens: bfloat16 [8, 8192, 4096], P('fsdp', 'seg')
- w_query: bfloat16 [4096, 2048], P(('seg', 'fsdp'))
- w_key: bfloat16 [4096, 512], P(('seg', 'fsdp'))
- value_weight: bfloat16 [4096, 512], P(('seg', 'fsdp')), may hold values from -0.09375 to 0.09375
- gate_bias: float32 [16], replicated, may hold values from -2 to 2
- block_mask: int32 [8, 32, 2, 2], P('fsdp', 'seg'), may hold values from 0 to 1, as said below
- valid_len: int32 [8, 32], P('fsdp', 'seg'), may hold values from 1 to 256, as said below
Outputs:
- attended: bfloat16 [8, 8192, 2048], P('fsdp', 'seg')
Inputs may be any that keep to these rules, and one draw needn't show every extreme that they name: block_mask[b, s] is 1 on its diagonal, 0 above it, and 0 or 1 below it. `valid_len`: the first segment of every book is full.
All inputs are finite; a program needn't handle non-finite values.
Results may differ from a plain program's by a relative error of at most 0.0095.
Values may be sent and summed in bfloat16 or wider, within the bound.
A program may use at most 128 MiB of HBM per device.

v0:
```python
import jax
import jax.numpy as jnp
from jax import lax
from jax.sharding import PartitionSpec as P

HEAD_SIZE = 128
BLK = 128


def carried_in(array, axis, combine, identity):
    length, here = (lax.axis_size(axis), lax.axis_index(axis))
    everything = jax.tree.map(
        lambda part, kind: lax.all_gather(part.astype(kind), axis),
        array,
        (jnp.bfloat16, jnp.bfloat16),
    )
    start = jax.tree.map(
        lambda part, zero: jnp.broadcast_to(jnp.asarray(zero, part.dtype), part.shape),
        array,
        identity,
    )

    def lap(k, before):
        reached = k < here
        new = combine(
            before, jax.tree.map(lambda part, own: part[k].astype(own.dtype), everything, array)
        )
        return jax.tree.map(lambda a, b: jnp.where(reached, a, b), new, before)

    return lax.fori_loop(0, length, lap, start)


def sigma_plus(values):
    return jax.nn.elu(values) + 1.0


def segment_delta(keys, values, valid):
    length = keys.shape[0]
    heads_kv = keys.shape[1] // HEAD_SIZE
    live = (jnp.arange(length, dtype=jnp.int32) < valid)[:, None, None]
    sig_keys = jnp.where(
        live, sigma_plus(keys.reshape(length, heads_kv, HEAD_SIZE).astype(jnp.float32)), 0.0
    )
    delta_m = jnp.einsum(
        "jgd,jge->gde",
        sig_keys,
        values.reshape(length, heads_kv, HEAD_SIZE).astype(jnp.float32),
        precision=lax.Precision.HIGHEST,
    )
    delta_z = jnp.sum(sig_keys, axis=0)
    return (delta_m, delta_z)


def memory_before(keys, values, valid):
    delta_m, delta_z = segment_delta(keys, values, valid)

    def combine(earlier, later):
        return (earlier[0] + later[0], earlier[1] + later[1])

    identity = (jnp.zeros_like(delta_m), jnp.zeros_like(delta_z))
    memory, normalizer = carried_in((delta_m, delta_z), "seg", combine, identity)
    return (memory, normalizer)


def segment_output(queries, keys, values, gate_bias, mask_blocks, valid, memory, normalizer):
    length = queries.shape[0]
    heads_kv = memory.shape[0]
    group = queries.shape[1] // (heads_kv * HEAD_SIZE)
    nblocks = mask_blocks.shape[0]
    q_heads = queries.reshape(length, heads_kv, group, HEAD_SIZE)
    k_heads = keys.reshape(length, heads_kv, HEAD_SIZE)
    v_heads = values.reshape(length, heads_kv, HEAD_SIZE)
    scores = jnp.einsum(
        "igxd,jgd->gxij", q_heads, k_heads, preferred_element_type=jnp.float32
    ) * HEAD_SIZE ** (-0.5)
    full = jnp.broadcast_to(mask_blocks[:, None, :, None], (nblocks, BLK, nblocks, BLK)).reshape(
        length, length
    )
    pos = jnp.arange(length, dtype=jnp.int32)
    allowed = (full > 0) & (pos[None, :] <= pos[:, None]) & (pos[None, :] < valid)
    masked = jnp.where(allowed, scores, -1e30)
    top = jnp.max(masked, axis=-1, keepdims=True)
    expo = jnp.where(allowed, jnp.exp(masked - top), 0.0)
    total = jnp.maximum(jnp.sum(expo, axis=-1, keepdims=True), 1.0)
    weights = (expo / total).astype(jnp.bfloat16)
    local = jnp.einsum("gxij,jgd->igxd", weights, v_heads, preferred_element_type=jnp.float32)
    sig_q = sigma_plus(q_heads.astype(jnp.float32))
    numer = jnp.einsum("igxd,gde->igxe", sig_q, memory, precision=lax.Precision.HIGHEST)
    denom = jnp.einsum("igxd,gd->igx", sig_q, normalizer, precision=lax.Precision.HIGHEST) + 1.0
    gate = jax.nn.sigmoid(gate_bias).reshape(heads_kv, group)[None, :, :, None]
    mixed = gate * (numer / denom[..., None]) + (1.0 - gate) * local
    live = (pos < valid)[:, None, None, None]
    return jnp.where(live, mixed, 0.0).reshape(length, -1).astype(jnp.bfloat16)


def shards(tokens, w_query, w_key, value_weight, gate_bias, block_mask, valid_len):
    seg_tokens = tokens[0]
    mask_blocks = block_mask[0, 0]
    valid = valid_len[0, 0]

    def add_rows(piece):
        return jnp.dot(seg_tokens, piece, preferred_element_type=jnp.float32)

    q_sum = add_rows(lax.all_gather(w_query, ("seg", "fsdp"), axis=0, tiled=True))
    k_sum = add_rows(lax.all_gather(w_key, ("seg", "fsdp"), axis=0, tiled=True))
    v_sum = add_rows(lax.all_gather(value_weight, ("seg", "fsdp"), axis=0, tiled=True))
    keys = k_sum.astype(jnp.bfloat16)
    values = v_sum.astype(jnp.bfloat16)
    queries = q_sum.astype(jnp.bfloat16)
    memory, normalizer = memory_before(keys, values, valid)
    output = segment_output(
        queries, keys, values, gate_bias, mask_blocks, valid, memory, normalizer
    )
    return output[None]


def solution(mesh):
    in_specs = (
        P("fsdp", "seg", None),
        P(("seg", "fsdp"), None),
        P(("seg", "fsdp"), None),
        P(("seg", "fsdp"), None),
        P(),
        P("fsdp", "seg", None, None),
        P("fsdp", "seg"),
    )
    out_specs = P("fsdp", "seg", None)
    return jax.shard_map(shards, mesh=mesh, in_specs=in_specs, out_specs=out_specs, check_vma=False)
```

profile of v0, /device:TPU:1, one launch (start us, length us, event | category | flops | bytes accessed | tf_op | source)
XLA Modules:
  0.0 465.9 jit_solution(6795826982219625871)
XLA Ops:
  8.7 121.7 %all-gather.6.cloned.1.call-done = bf16[4096,512]{1,0:T(8,128)(2,1)} async-done(((bf16[16,512]{1,0:T(8,128)(2,1)}), bf16[4096,512]{1,0:T(8,128)(2,1)}) %all-gather.6.cloned.1.call-update) | async-done | bytes 4194320 | tf_op jit(solution)/shard_map/all_gather | solution.py:105
  130.4 3.6 fusion.42
  134.3 112.1 %all-gather.8.cloned.1.call-done = bf16[4096,512]{1,0:T(8,128)(2,1)} async-done(((bf16[16,512]{1,0:T(8,128)(2,1)}), bf16[4096,512]{1,0:T(8,128)(2,1)}) %all-gather.8.cloned.1.call-update) | async-done | bytes 4194320 | tf_op jit(solution)/shard_map/all_gather | solution.py:106
  246.4 3.4 fusion.28
  249.8 1.3 convolution_convert_fusion.1
  253.0 23.6 %all_gather.23 = bf16[32,4,128]{2,1,0:T(4,128)(2,1)S(1)} all-gather(bf16[1,4,128]{2,1,0:T(4,128)(2,1)S(1)} %bitcast.97), channel_id=1, replica_groups=mesh['seg'=32,'fsdp'=8] {'seg'}, dimensions={0}, use_global_device_ids=true | all-gather | bytes 33792 | tf_op jit(solution)/shard_map/all_gather | solution.py:13
  276.7 22.9 %all-gather.12.cloned.1.call-done = bf16[128,128,128]{2,1,0:T(8,128)(2,1)} async-done(((bf16[4,128,128]{2,1,0:T(8,128)(2,1)}), bf16[128,128,128]{2,1,0:T(8,128)(2,1)}) %all-gather.12.cloned.1.call-update) | async-done | bytes 4194320 | tf_op jit(solution)/shard_map/all_gather | solution.py:13
  299.6 34.6 %while.16 = (s32[]{:T(128)}, f32[4,128,128]{2,1,0:T(8,128)S(1)}, f32[4,128]{1,0:T(4,128)S(1)}, s32[]{:T(128)}, bf16[32,4,128,128]{3,2,1,0:T(8,128)(2,1)}, /*inde...) while((s32[]{:T(128)}, f32[4,128,128]{2,1,0:T(8,128)S(1)}, f32[4,128]{1,0:T(4,128)S(1)}, ...), condition=%wide.region_2.3_spmd.clone, body=%wide.region_1.2_spmd.clone.sunk | while | flops 264196 | bytes 660603 | solution.py:30
  300.7 1.0 add_select_fusion.4
  301.8 1.0 add_select_fusion.4
  302.9 1.0 add_select_fusion.4
  303.9 1.0 add_select_fusion.4
  305.0 1.0 add_select_fusion.4
  306.1 1.0 add_select_fusion.4
  307.2 1.0 add_select_fusion.4
  308.3 1.0 add_select_fusion.4
  309.4 1.0 add_select_fusion.4
  310.4 1.0 add_select_fusion.4
  311.5 1.0 add_select_fusion.4
  312.6 1.0 add_select_fusion.4
  313.7 1.0 add_select_fusion.4
  314.8 1.0 add_select_fusion.4
  315.9 1.0 add_select_fusion.4
  316.9 1.0 add_select_fusion.4
  318.0 1.0 add_select_fusion.4
  319.1 1.0 add_select_fusion.4
  320.2 1.0 add_select_fusion.4
  321.3 1.0 add_select_fusion.4
  322.4 1.0 add_select_fusion.4
  323.4 1.0 add_select_fusion.4
  324.5 1.0 add_select_fusion.4
  325.6 1.0 add_select_fusion.4
  326.7 1.0 add_select_fusion.4
  327.8 1.0 add_select_fusion.4
  328.9 1.0 add_select_fusion.4
  329.9 1.0 add_select_fusion.4
  331.0 1.0 add_select_fusion.4
  332.1 1.0 add_select_fusion.4
  333.2 1.0 add_select_fusion.4
  334.2 93.2 %all-gather.10.cloned.1.call-done = bf16[4096,2048]{1,0:T(8,128)(2,1)} async-done(((bf16[16,2048]{1,0:T(8,128)(2,1)}), bf16[4096,2048]{1,0:T(8,128)(2,1)}) %all-gather.10.cloned.1.call-update) | async-done | bytes 16777232 | tf_op jit(solution)/shard_map/all_gather | solution.py:104
  427.4 9.2 %convolution_convert_fusion = bf16[256,2048]{1,0:T(8,128)(2,1)} fusion(bf16[4096,2048]{1,0:T(8,128)(2,1)} %all-gather.10.cloned.1.call-done, bf16[1,256,4096]{2,1,0:T(8,128)(2,1)S(1)} %copy-done), kind=kOutput, calls=%fused_computation.9 | convolution fusion | flops 4295491584 | bytes 19922944 | tf_op jit(solution)/shard_map/dot_general | solution.py:102
  436.6 1.5 copy.54
  438.1 5.2 %fusion.20 = f32[4,1,256,4]{1,2,3,0:T(8,128)} fusion(f32[4,128,1,1]{1,2,3,0:T(1,128)S(1)} %bitcast.96, bf16[256,4,4,128]{0,3,2,1:T(8,128)(2,1)S(1)} %bitcast.88), kind=kOutput, calls=%fused_computation.32 | convolution fusion | flops 8916992 | bytes 1067008 | tf_op jit(solution)/shard_map/igxd,gd->igx/dot_general | solution.py:89
  443.3 2.2 copy.57
  445.5 4.7 %fusion.69 = (f32[4,4,256]{2,1,0:T(4,128)S(1)}, f32[4,4,256,256]{2,3,1,0:T(8,128)}) fusion(pred[256,256]{0,1:T(8,128)(4,1)S(1)} %copy.35, bf16[256,4,4,128]{0,3,2,1:T(8,128)(2,1)S(1)} %bitcast.89, bf16[256,4,128,1]{2,1,0,3:T(4,128)(2,1)} %bitcast.92), kind=kOutput, calls=%fused_computation.76 | convolution fusion | flops 273678592 | bytes 5586944 | tf_op jit(solution)/shard_map/sub | solution.py:83
  450.2 2.8 fusion.14
  453.1 4.1 fusion.5
  457.1 2.3 copy.40
  (64 shorter events, 5.1 us)
Async XLA Ops:
  6.5 123.8 %copy-start = (bf16[1,256,4096]{2,1,0:T(8,128)(2,1)S(1)}, bf16[1,256,4096]{2,1,0:T(8,128)(2,1)}, u32[]{:S(2)}) copy-start(bf16[1,256,4096]{2,1,0:T(8,128)(2,1)} %param.9) | copy-start | bytes 6291460
  6.5 123.8 %all-gather.6.cloned.1.call-start = ((), (), s32[]{:S(2)}) async-start(), calls=%async_computation | async-start | bytes 4210688 | tf_op jit(solution)/shard_map/all_gather | solution.py:105
  7.3 239.1 %all-gather.8.cloned.1.call-start = ((), (), s32[]{:S(2)}) async-start(), calls=%async_computation.1 | async-start | bytes 4210688 | tf_op jit(solution)/shard_map/all_gather | solution.py:106
  8.0 291.6 %all-gather.12.cloned.1.call-start = ((), (), s32[]{:S(2)}) async-start(), calls=%async_computation.3 | async-start | bytes 4325376 | tf_op jit(solution)/shard_map/all_gather | solution.py:13
  134.1 115.7 %copy-start.1 = (bf16[256,4,128]{2,1,0:T(4,128)(2,1)}, bf16[256,4,128]{2,1,0:T(4,128)(2,1)S(1)}, u32[]{:S(2)}) copy-start(bf16[256,4,128]{2,1,0:T(4,128)(2,1)S(1)} %reshape.73) | copy-start | bytes 786436
  134.3 117.5 %copy-start.3 = (f32[16]{0:T(128)S(1)}, f32[16]{0:T(128)}, u32[]{:S(2)}) copy-start(f32[16]{0:T(128)} %param.13) | copy-start | bytes 196
  134.3 117.6 %copy-start.2 = (s32[1,1,2,2]{3,2,1,0:T(2,128)S(1)}, s32[1,1,2,2]{3,2,1,0:T(2,128)}, u32[]{:S(2)}) copy-start(s32[1,1,2,2]{3,2,1,0:T(2,128)} %param.14) | copy-start | bytes 52
  251.1 176.3 %all-gather.10.cloned.1.call-start = ((), (), s32[]{:S(2)}) async-start(), calls=%async_computation.2 | async-start | bytes 16842752 | tf_op jit(solution)/shard_map/all_gather | solution.py:104
Sparse Core Ops, SparseCore 0:
  11.0 119.3 all-gather.5
  134.0 112.3 all-gather.7
  251.3 48.3 all-gather.11
  303.1 124.3 all-gather.9
where the time goes:
time: 467 us; the launch traced here: 466 us
  waiting for transfers between devices  352 us (75%)
  matrix products  34.3 us (7%)
  other arithmetic  33.9 us (7%)
  blocking collectives  23.6 us (5%)
  between operations  13.9 us (3%)
  local copies, waits for them, and re-layouts  7.38 us (2%)
    all_gather x1, waiting for transfers between devices, shards(): k_sum = add_rows(lax.all_gather(w_key, ('seg', 'fsdp'), axis=0, tiled=True))  122 us
    all_gather x1, waiting for transfers between devices, shards(): lax.all_gather(value_weight, ('seg', 'fsdp'), axis=0, tiled=True)  112 us
    all_gather x1, waiting for transfers between devices, shards(): lax.all_gather(w_query, ('seg', 'fsdp'), axis=0, tiled=True)  93.2 us
    select_n x64, other arithmetic, lap(): return jax.tree.map(lambda a, b: jnp.where(reached, a, b), new, before)  33.8 us
    all_gather x1, blocking collectives, carried_in(): lax.all_gather(part.astype(kind), axis)  23.6 us
    all_gather x1, waiting for transfers between devices, carried_in(): lax.all_gather(part.astype(kind), axis)  22.9 us
    dot_general x3, matrix products, add_rows(): return jnp.dot(seg_tokens, piece, preferred_element_type=jnp.float32)  16.3 us
  transfers between devices with their start and end apart: 4, of which 4 were waited for; matrix products, arithmetic and copies ran while one was open for 8% of the time, Pallas kernels for 0%

commit v1 on v0

--- a/solution.py
+++ b/solution.py
@@ -103,7 +103,14 @@
 
     q_sum = add_rows(lax.all_gather(w_query, ("seg", "fsdp"), axis=0, tiled=True))
     k_sum = add_rows(lax.all_gather(w_key, ("seg", "fsdp"), axis=0, tiled=True))
-    v_sum = add_rows(lax.all_gather(value_weight, ("seg", "fsdp"), axis=0, tiled=True))
+
+    def answer_the_series_all(shard_in, net_axis):
+        piece_now = jnp.stack([shard_in for _ in range(jax.lax.axis_size(net_axis))])
+        vec_out = jax.lax.all_to_all(piece_now, axis_name=net_axis, split_axis=0, concat_axis=0)
+        x_now = jnp.concatenate(vec_out, axis=0)
+        return x_now
+
+    v_sum = add_rows(answer_the_series_all(value_weight, ("seg", "fsdp")))
     keys = k_sum.astype(jnp.bfloat16)
     values = v_sum.astype(jnp.bfloat16)
     queries = q_sum.astype(jnp.bfloat16)

time: 467 us -> 369 us (0.79)
  waiting for transfers between devices: 352 us -> 233 us
  starting transfers between devices: 0.12 us -> 16.7 us
    all_gather x1 -> x0, waiting for transfers between devices: 112 us -> none  [shards(): lax.all_gather(value_weight, ('seg', 'fsdp'), axis=0, tiled=True)]
    all_to_all x0 -> x1, starting transfers between devices: none -> 16.7 us  [answer_the_series_all(): jax.lax.all_to_all(piece_now, axis_name=net_axis, split_axis=0, concat_ax...]
    all_gather x1, waiting for transfers between devices: 122 us -> 115 us  [shards(): k_sum = add_rows(lax.all_gather(w_key, ('seg', 'fsdp'), axis=0, tiled=True))]
  transfers between devices with their start and end apart: 4 -> 4, of which waited for: 4 -> 3; matrix products, arithmetic and copies ran while one was open for 8% -> 11% of each run, Pallas kernels for 0% -> 0%
where the time goes in v1:
time: 369 us; the launch traced here: 368 us
  waiting for transfers between devices  233 us (63%)
  matrix products  34.3 us (9%)
  other arithmetic  33.9 us (9%)
  blocking collectives  24.8 us (7%)
  starting transfers between devices  16.7 us (5%)
  between operations  13.9 us (4%)
  local copies, waits for them, and re-layouts  10.6 us (3%)
    all_gather x1, waiting for transfers between devices, shards(): k_sum = add_rows(lax.all_gather(w_key, ('seg', 'fsdp'), axis=0, tiled=True))  115 us
    all_gather x1, waiting for transfers between devices, shards(): lax.all_gather(w_query, ('seg', 'fsdp'), axis=0, tiled=True)  93.3 us
    select_n x64, other arithmetic, lap(): return jax.tree.map(lambda a, b: jnp.where(reached, a, b), new, before)  33.8 us
    all_gather x1, blocking collectives, carried_in(): lax.all_gather(part.astype(kind), axis)  24.8 us
    all_gather x1, waiting for transfers between devices, carried_in(): lax.all_gather(part.astype(kind), axis)  22.7 us
    all_to_all x1, starting transfers between devices, answer_the_series_all(): jax.lax.all_to_all(piece_now, axis_name=net_axis, split_axis=0, concat_ax...  16.7 us
    dot_general x3, matrix products, add_rows(): return jnp.dot(seg_tokens, piece, preferred_element_type=jnp.float32)  16.3 us
  transfers between devices with their start and end apart: 4, of which 3 were waited for; matrix products, arithmetic and copies ran while one was open for 11% of the time, Pallas kernels for 0%

profile of v1, /device:TPU:1, one launch (start us, length us, event | category | flops | bytes accessed | tf_op | source)
XLA Modules:
  0.0 367.9 jit_solution(13849976453319017268)
XLA Ops:
  7.3 3.2 stack.2
  10.5 16.7 %all-to-all-start = ((bf16[256,16,512]{2,1,0:T(8,128)(2,1)}), bf16[256,16,512]{2,1,0:T(8,128)(2,1)}, u32[]{:S(2)}, u32[]{:S(2)}) async-start(bf16[256,16,512]{2,1,0:T(8,128)(2,1)} %stack.2), calls=%async_computation | async-start | bytes 8388608 | tf_op jit(solution)/shard_map/all_to_all | solution.py:109
  27.9 115.4 %all-gather.5.cloned.1.call-done = bf16[4096,512]{1,0:T(8,128)(2,1)} async-done(((bf16[16,512]{1,0:T(8,128)(2,1)}), bf16[4096,512]{1,0:T(8,128)(2,1)}) %all-gather.5.cloned.1.call-update) | async-done | bytes 4194320 | tf_op jit(solution)/shard_map/all_gather | solution.py:105
  143.2 3.6 fusion.42
  147.2 3.4 fusion.28
  150.6 1.3 convolution_convert_fusion.1
  154.0 24.8 %all_gather.19 = bf16[32,4,128]{2,1,0:T(4,128)(2,1)S(1)} all-gather(bf16[1,4,128]{2,1,0:T(4,128)(2,1)S(1)} %bitcast.98), channel_id=1, replica_groups=mesh['seg'=32,'fsdp'=8] {'seg'}, dimensions={0}, use_global_device_ids=true | all-gather | bytes 33792 | tf_op jit(solution)/shard_map/all_gather | solution.py:13
  178.8 22.7 %all-gather.9.cloned.1.call-done = bf16[128,128,128]{2,1,0:T(8,128)(2,1)} async-done(((bf16[4,128,128]{2,1,0:T(8,128)(2,1)}), bf16[128,128,128]{2,1,0:T(8,128)(2,1)}) %all-gather.9.cloned.1.call-update) | async-done | bytes 4194320 | tf_op jit(solution)/shard_map/all_gather | solution.py:13
  201.5 34.6 %while.16 = (s32[]{:T(128)}, f32[4,128,128]{2,1,0:T(8,128)S(1)}, f32[4,128]{1,0:T(4,128)S(1)}, s32[]{:T(128)}, bf16[32,4,128,128]{3,2,1,0:T(8,128)(2,1)}, /*inde...) while((s32[]{:T(128)}, f32[4,128,128]{2,1,0:T(8,128)S(1)}, f32[4,128]{1,0:T(4,128)S(1)}, ...), condition=%wide.region_2.3_spmd.clone, body=%wide.region_1.2_spmd.clone.sunk | while | flops 264196 | bytes 660603 | solution.py:30
  202.6 1.0 add_select_fusion.4
  203.7 1.0 add_select_fusion.4
  204.8 1.0 add_select_fusion.4
  205.8 1.0 add_select_fusion.4
  206.9 1.0 add_select_fusion.4
  208.0 1.0 add_select_fusion.4
  209.1 1.0 add_select_fusion.4
  210.2 1.0 add_select_fusion.4
  211.3 1.0 add_select_fusion.4
  212.3 1.0 add_select_fusion.4
  213.4 1.0 add_select_fusion.4
  214.5 1.0 add_select_fusion.4
  215.6 1.0 add_select_fusion.4
  216.7 1.0 add_select_fusion.4
  217.8 1.0 add_select_fusion.4
  218.8 1.0 add_select_fusion.4
  219.9 1.0 add_select_fusion.4
  221.0 1.0 add_select_fusion.4
  222.1 1.0 add_select_fusion.4
  223.2 1.0 add_select_fusion.4
  224.3 1.0 add_select_fusion.4
  225.3 1.0 add_select_fusion.4
  226.4 1.0 add_select_fusion.4
  227.5 1.0 add_select_fusion.4
  228.6 1.0 add_select_fusion.4
  229.7 1.0 add_select_fusion.4
  230.8 1.0 add_select_fusion.4
  231.8 1.0 add_select_fusion.4
  232.9 1.0 add_select_fusion.4
  234.0 1.0 add_select_fusion.4
  236.1 93.3 %all-gather.7.cloned.1.call-done = bf16[4096,2048]{1,0:T(8,128)(2,1)} async-done(((bf16[16,2048]{1,0:T(8,128)(2,1)}), bf16[4096,2048]{1,0:T(8,128)(2,1)}) %all-gather.7.cloned.1.call-update) | async-done | bytes 16777232 | tf_op jit(solution)/shard_map/all_gather | solution.py:104
  329.5 9.2 %convolution_convert_fusion = bf16[256,2048]{1,0:T(8,128)(2,1)} fusion(bf16[4096,2048]{1,0:T(8,128)(2,1)} %all-gather.7.cloned.1.call-done, bf16[1,256,4096]{2,1,0:T(8,128)(2,1)S(1)} %copy-done), kind=kOutput, calls=%fused_computation.9 | convolution fusion | flops 4295491584 | bytes 19922944 | tf_op jit(solution)/shard_map/dot_general | solution.py:102
  338.7 1.5 copy.54
  340.1 4.7 %fusion.69 = (f32[4,4,256]{2,1,0:T(4,128)S(1)}, f32[4,4,256,256]{2,3,1,0:T(8,128)}) fusion(pred[256,256]{0,1:T(8,128)(4,1)S(1)} %copy.35, bf16[256,4,4,128]{0,3,2,1:T(8,128)(2,1)S(1)} %bitcast.89, bf16[256,4,128,1]{2,1,0,3:T(4,128)(2,1)} %bitcast.93), kind=kOutput, calls=%fused_computation.76 | convolution fusion | flops 273678592 | bytes 5586944 | tf_op jit(solution)/shard_map/sub | solution.py:83
  344.8 5.2 %fusion.20 = f32[4,1,256,4]{1,2,3,0:T(8,128)} fusion(f32[4,128,1,1]{1,2,3,0:T(1,128)S(1)} %bitcast.97, bf16[256,4,4,128]{0,3,2,1:T(8,128)(2,1)S(1)} %bitcast.90), kind=kOutput, calls=%fused_computation.32 | convolution fusion | flops 8916992 | bytes 1067008 | tf_op jit(solution)/shard_map/igxd,gd->igx/dot_general | solution.py:89
  350.0 2.2 copy.57
  352.2 2.8 fusion.14
  355.1 4.1 %fusion.5 = bf16[256,4,4,128]{0,3,2,1:T(8,128)(2,1)} fusion(f32[4,128,4,256]{3,1,2,0:T(8,128)S(1)} %fusion.14, bf16[256,4,4,128]{0,3,2,1:T(8,128)(2,1)S(1)} %bitcast.91, f32[4,4]{1,0:T(4,128)S(1)} %broadcast_subtract_fusion, f32[256,4,4]{0,2,1:T(4,128)S(1)} %bitcast_bitcast_fusion, f32[4,4]{1,0:T(4,128)S(1)} %mul.30, ...), kind=kOutput, calls=%fused_computation.14 | convolution fusion | flops 811073536 | bytes 4473216 | tf_op jit(solution)/shard_map/igxd,gde->igxe/dot_general | solution.py:88
  359.1 2.3 copy.40
  (64 shorter events, 5.6 us)
Async XLA Ops:
  6.5 136.7 %copy-start = (bf16[1,256,4096]{2,1,0:T(8,128)(2,1)S(1)}, bf16[1,256,4096]{2,1,0:T(8,128)(2,1)}, u32[]{:S(2)}) copy-start(bf16[1,256,4096]{2,1,0:T(8,128)(2,1)} %param.9) | copy-start | bytes 6291460
  6.5 136.7 %all-gather.5.cloned.1.call-start = ((), (), s32[]{:S(2)}) async-start(), calls=%async_computation.1 | async-start | bytes 4210688 | tf_op jit(solution)/shard_map/all_gather | solution.py:105
  10.5 136.6 %all-to-all-start = ((bf16[256,16,512]{2,1,0:T(8,128)(2,1)}), bf16[256,16,512]{2,1,0:T(8,128)(2,1)}, u32[]{:S(2)}, u32[]{:S(2)}) async-start(bf16[256,16,512]{2,1,0:T(8,128)(2,1)} %stack.2), calls=%async_computation | async-start | bytes 8388608 | tf_op jit(solution)/shard_map/all_to_all | solution.py:109
  27.1 174.4 %all-gather.9.cloned.1.call-start = ((), (), s32[]{:S(2)}) async-start(), calls=%async_computation.3 | async-start | bytes 4325376 | tf_op jit(solution)/shard_map/all_gather | solution.py:13
  146.9 3.7 copy-start.1
  147.1 5.5 %copy-start.3 = (f32[16]{0:T(128)S(1)}, f32[16]{0:T(128)}, u32[]{:S(2)}) copy-start(f32[16]{0:T(128)} %param.13) | copy-start | bytes 196
  147.2 5.6 %copy-start.2 = (s32[1,1,2,2]{3,2,1,0:T(2,128)S(1)}, s32[1,1,2,2]{3,2,1,0:T(2,128)}, u32[]{:S(2)}) copy-start(s32[1,1,2,2]{3,2,1,0:T(2,128)} %param.14) | copy-start | bytes 52
  151.9 177.6 %all-gather.7.cloned.1.call-start = ((), (), s32[]{:S(2)}) async-start(), calls=%async_computation.2 | async-start | bytes 16842752 | tf_op jit(solution)/shard_map/all_gather | solution.py:104
Sparse Core Ops, SparseCore 0:
  11.0 132.2 all-gather.4
  152.0 49.4 all-gather.8
  205.1 124.3 all-gather.6
